TPU v7x, 32 devices: a whole 2x2x4 slice. The times are simulated.
32 devices in a mesh: section: 2 (over x), view: 8 (over z, y), scene: 2 (over core).
Axes of the slice: x: 2, y: 2, z: 4, core: 2. Of those that a mesh axis runs over, the one named last changes fastest.
Arguments:
- tokens: bfloat16 [2, 512, 1024], P('scene', ('section', 'view')), may hold values from -6 to 6
- norm_gain: float32 [1024], replicated, may hold values from 0.1 to 1.9
- head_weight: bfloat16 [1024, 512], replicated, may hold values from -0.1875 to 0.1875
- tile_lists: int32 [2, 64, 128], P('scene', ('section', 'view')), may hold values from 0 to 32767, as said below
- tile_counts: int32 [2, 64], P('scene', ('section', 'view')), may hold values from 1 to 128, as said below
- cameras: float32 [2, 2, 8], P('scene'), may hold values from -3 to 3
- targets: bfloat16 [2, 64, 768], P('scene', ('section', 'view')), may hold values from 0 to 1
Outputs:
- image: bfloat16 [2, 64, 768], P('scene', ('section', 'view'))
- grad_head: float32 [1024, 512], replicated
- loss: float32 [], replicated
Inputs may be any that keep to these rules, and one draw needn't show every extreme that they name: `tile_lists`: gaussian n of a scene has owner n // 2048. Among the 512 slots (live or not) of each aligned block of 4 tiles, at most 64 name Gaussians of one owner, and in every such block some owner is named exactly 64 times. `tile_counts`: the first tile of each scene has 128 live slots.
All inputs are finite; a program needn't handle non-finite values.
Results may differ from a plain program's by a relative error of at most 0.014.
Values may be sent and summed in bfloat16 or wider, within the bound.
A program may use at most 256 MiB of HBM per device.

v0:
```python
import jax
import jax.numpy as jnp
from jax import lax
from jax.sharding import PartitionSpec as P

GPT = 64
PARAMS = 8
K = 128
SIDE = 16
VIEWS = 2


def pixel_grid():
    place = jnp.arange(SIDE * SIDE, dtype=jnp.int32)
    across = ((place % SIDE).astype(jnp.float32) + 0.5) * (2.0 / SIDE) - 1.0
    down = ((place // SIDE).astype(jnp.float32) + 0.5) * (2.0 / SIDE) - 1.0
    return (across, down)


def composite(values, live, cams, wanted, across, down):
    slots = jnp.arange(K, dtype=jnp.int32)
    strict = (slots[:, None] < slots[None, :]).astype(jnp.float32)
    sx = jnp.tanh(
        cams[:, 0:1] * values[0]
        + cams[:, 1:2] * values[1]
        + cams[:, 2:3] * values[2]
        + cams[:, 3:4]
    )
    sy = jnp.tanh(
        cams[:, 4:5] * values[0]
        + cams[:, 5:6] * values[1]
        + cams[:, 6:7] * values[2]
        + cams[:, 7:8]
    )
    spread = jnp.exp(-2.0 * values[3])
    dxx = across[None, None, :] - sx[:, :, None]
    dyy = down[None, None, :] - sy[:, :, None]
    alpha = (
        0.3
        * jax.nn.sigmoid(values[4])[:, :, None]
        * jnp.exp(-0.5 * (dxx * dxx + dyy * dyy) * spread[:, :, None])
        * live[:, :, None]
    )
    logs = jnp.log1p(-alpha)
    before = jnp.einsum("bkp,kj->bjp", logs, strict, precision=lax.Precision.HIGHEST)
    weight = alpha * jnp.exp(before)
    colour = jnp.einsum(
        "bkp,cbk->bcp", weight, jax.nn.sigmoid(values[5:8]), precision=lax.Precision.HIGHEST
    )
    colour = colour.reshape(colour.shape[0], 3 * SIDE * SIDE)
    diff = colour - wanted.astype(jnp.float32)
    return (jnp.sum(diff * diff), colour)


def to_gauss(head, rows):
    return (
        head.reshape(rows, PARAMS, GPT)
        .transpose(1, 0, 2)
        .reshape(PARAMS, rows * GPT)
        .astype(jnp.bfloat16)
    )


def body(tokens, norm_gain, head_weight, tile_lists, tile_counts, cameras, targets):
    tok_rows = tokens.shape[1]
    tile_rows = tile_lists.shape[1]
    group = lax.axis_size(("section", "view"))
    scenes_all = lax.axis_size("scene")
    tiles_all = tile_rows * group
    factor = 1.0 / (scenes_all * tiles_all)
    values_in = tokens[0].astype(jnp.float32)
    scale = lax.rsqrt(jnp.mean(values_in * values_in, axis=-1, keepdims=True) + 1e-06)
    normed = (values_in * scale * norm_gain).astype(jnp.bfloat16)
    lists = tile_lists[0]
    own_count = tok_rows * GPT
    slot_total = tile_rows * K
    bucket = 2 * ((slot_total + group - 1) // group)
    flat = lists.reshape(-1)
    owner = flat // own_count
    inner = flat - owner * own_count
    order = jnp.argsort(owner, stable=True)
    sorted_owner = owner[order]
    owner_ids = jnp.arange(group, dtype=jnp.int32)
    per_owner = jnp.sum((owner[:, None] == owner_ids[None, :]).astype(jnp.int32), axis=0)
    starts = jnp.cumsum(per_owner) - per_owner
    rank = jnp.arange(slot_total, dtype=jnp.int32) - starts[sorted_owner]
    target_slot = jnp.zeros((slot_total,), jnp.int32).at[order].set(sorted_owner * bucket + rank)
    wanted_rows = (
        jnp.zeros((group * bucket,), jnp.int32).at[target_slot].set(inner).reshape(group, bucket)
    )
    asked = lax.all_to_all(
        wanted_rows, ("section", "view"), split_axis=0, concat_axis=0, tiled=True
    )
    head = jnp.dot(normed, head_weight, preferred_element_type=jnp.float32)
    own_gauss = to_gauss(head, tok_rows)
    answer = (
        jnp.take(own_gauss, asked.reshape(-1), axis=1)
        .reshape(PARAMS, group, bucket)
        .transpose(1, 0, 2)
    )
    received = lax.all_to_all(answer, ("section", "view"), split_axis=0, concat_axis=0, tiled=True)
    table = received.transpose(1, 0, 2).reshape(PARAMS, group * bucket).astype(jnp.float32)
    values = jnp.take(table, target_slot, axis=1).reshape(PARAMS, tile_rows, K)
    per_view = tiles_all // VIEWS
    first_tile = lax.axis_index(("section", "view")) * tile_rows
    which = (first_tile + jnp.arange(tile_rows, dtype=jnp.int32)) // per_view
    onehot = (which[:, None] == jnp.arange(VIEWS, dtype=jnp.int32)[None, :]).astype(jnp.float32)
    tile_cams = jnp.dot(onehot, cameras[0], precision=lax.Precision.HIGHEST)
    slots = jnp.arange(K, dtype=jnp.int32)
    live = (slots[None, :] < tile_counts[0][:, None]).astype(jnp.float32)
    across, down = pixel_grid()

    def local(vals):
        return composite(vals, live, tile_cams, targets[0], across, down)

    part, pullback, colour = jax.vjp(local, values, has_aux=True)
    grads = pullback(jnp.ones_like(part) * factor)[0]
    outgoing = (
        jnp.zeros((PARAMS, group * bucket), jnp.float32)
        .at[:, target_slot]
        .set(grads.reshape(PARAMS, -1))
    )
    outgoing = outgoing.reshape(PARAMS, group, bucket).transpose(1, 0, 2)
    returned = lax.all_to_all(
        outgoing.astype(jnp.bfloat16), ("section", "view"), split_axis=0, concat_axis=0, tiled=True
    ).astype(outgoing.dtype)
    own = (
        jnp.zeros((PARAMS, own_count), jnp.float32)
        .at[:, asked.reshape(-1)]
        .add(returned.transpose(1, 0, 2).reshape(PARAMS, -1))
    )
    dhead = own.reshape(PARAMS, tok_rows, GPT).transpose(1, 0, 2).reshape(tok_rows, PARAMS * GPT)
    partial_grad = jnp.dot(normed.astype(jnp.float32).T, dhead, precision=lax.Precision.HIGHEST)
    grad_head, loss = lax.psum((partial_grad, part * factor), ("section", "view", "scene"))
    return (colour.astype(jnp.bfloat16)[None], grad_head, loss)


def solution(mesh):
    in_specs = (
        P("scene", ("section", "view"), None),
        P(),
        P(),
        P("scene", ("section", "view"), None),
        P("scene", ("section", "view")),
        P("scene", None, None),
        P("scene", ("section", "view"), None),
    )
    out_specs = (P("scene", ("section", "view"), None), P(), P())
    return jax.shard_map(body, mesh=mesh, in_specs=in_specs, out_specs=out_specs, check_vma=False)
```

profile of v0, /device:TPU:0, one launch (start us, length us, event | category | flops | bytes accessed | tf_op | source)
XLA Modules:
  0.0 234.9 jit_solution(6555050550553904931)
XLA Ops:
  7.2 0.8 bitcast_subtract_fusion
  8.1 3.8 %sort.17 = (s32[512]{0:T(512)}, s32[512]{0:T(512)S(1)}) sort(s32[512]{0:T(512)S(1)} %get-tuple-element.51, s32[512]{0:T(512)S(1)} %iota.50), dimensions={0}, to_apply=%region_0.0 | sort | flops 4608 | bytes 8192 | tf_op jit(solution)/shard_map/jit(argsort)/sort | solution.py:81
  11.9 3.5 %gather_fusion = s32[512]{0:T(512)S(1)} fusion(s32[512]{0:T(512)S(1)} %get-tuple-element.51, s32[1024]{0:T(1024)S(1)} %pad_clamp_fusion.1), kind=kCustom, calls=%fused_computation | custom fusion | bytes 6144 | tf_op jit(solution)/shard_map/gather | solution.py:82
  15.7 0.7 fusion.106
  16.4 4.3 %compare_select_fusion.3 = (s32[512,1]{0,1:T(1,128)S(1)}, s32[512,1]{0,1:T(1,128)S(1)}) fusion(s32[]{:T(128)} %bitcast.12, s32[]{:T(128)} %bitcast.13, s32[]{:T(128)} %bitcast.14, s32[]{:T(128)} %bitcast.15, s32[]{:T(128)} %bitcast.16, s32[]{:T(128)} %bitcast.18, s32[]{:T(128)} %bitcast.17, s32[512,1]{0,1:T(1,128)S(1)} %bitcast.179), kind=kLoop, calls=%fused_computation.113 | loop fusion | flops 7680 | bytes 6172 | tf_op jit(solution)/shard_map/gather | solution.py:86
  20.8 5.7 %fusion.82 = s32[512]{0:T(512)S(1)} fusion(pred[512]{0:T(512)(128)(4,1)S(1)} %get-tuple-element.25, pred[512]{0:T(512)(128)(4,1)S(1)} %get-tuple-element.24, pred[512]{0:T(512)(128)(4,1)S(1)} %get-tuple-element.23, pred[512]{0:T(512)(128)(4,1)S(1)} %get-tuple-element.22, pred[512]{0:T(512)(128)(4,1)S(1)} %get-tuple-element.21, ...), kind=kLoop, calls=%fused_computation.148 | loop fusion | flops 6144 | bytes 10788 | tf_op jit(solution)/shard_map/add | solution.py:87
  26.5 2.4 %scatter_custom_fusion = s32[512]{0:T(512)S(1)} fusion(s32[512]{0:T(512)S(1)} %compare_select_fusion.10, s32[512]{0:T(512)S(1)} %fusion.82, s32[]{:T(128)} %constant.112.clone.1), kind=kCustom, calls=%fused_computation.196 | custom fusion | bytes 2052 | tf_op jit(solution)/shard_map/scatter | solution.py:87
  29.0 2.4 %scatter_custom_fusion.1 = s32[1024]{0:T(1024)S(1)} fusion(s32[512]{0:T(512)S(1)} %compare_select_fusion.9, s32[512]{0:T(512)S(1)} %get-tuple-element.50, s32[]{:T(128)} %constant.112.clone.1), kind=kCustom, calls=%fused_computation.162 | custom fusion | bytes 4100 | tf_op jit(solution)/shard_map/scatter | solution.py:89
  31.4 0.7 all_to_all.12
  32.1 8.3 %all-to-all-start = ((s32[16,1,64]{2,1,0:T(1,128)}), s32[16,1,64]{2,1,0:T(1,128)S(1)}, u32[]{:S(2)}, u32[]{:S(2)}) async-start(s32[16,1,64]{2,1,0:T(1,128)} %all_to_all.12), calls=%async_computation | async-start | bytes 16384 | tf_op jit(solution)/shard_map/all_to_all | solution.py:91
  41.3 0.5 copy.122
  41.9 0.6 fusion.4
  42.8 4.9 %all-to-all-done = s32[16,1,64]{2,1,0:T(1,128)S(1)} async-done(((s32[16,1,64]{2,1,0:T(1,128)}), s32[16,1,64]{2,1,0:T(1,128)S(1)}, u32[]{:S(2)}, u32[]{:S(2)}) %all-to-all-start) | async-done | bytes 4128 | tf_op jit(solution)/shard_map/all_to_all | solution.py:91
  48.2 0.7 reduce.40
  49.0 3.2 %gather_fusion.1 = bf16[1024,8]{1,0:T(8,128)(2,1)S(1)} fusion(bf16[8,2048]{0,1:T(8,128)(2,1)S(1)} %bitcast.162, s32[1024]{0:T(1024)S(1)} %broadcast_clamp_fusion), kind=kCustom, calls=%fused_computation.1 | custom fusion | bytes 36864 | tf_op jit(solution)/shard_map/jit(_take)/gather | solution.py:97
  52.4 0.7 reshape.1807
  53.1 3.5 %all-to-all-start.1 = ((bf16[16,2,256]{2,1,0:T(2,128)(2,1)}), bf16[16,2,256]{2,1,0:T(2,128)(2,1)S(1)}, u32[]{:S(2)}, u32[]{:S(2)}) async-start(bf16[16,2,256]{2,1,0:T(2,128)(2,1)} %reshape.1807), calls=%async_computation.1 | async-start | bytes 32768 | tf_op jit(solution)/shard_map/all_to_all | solution.py:101
  56.7 7.2 %all-to-all-done.1 = bf16[16,2,256]{2,1,0:T(2,128)(2,1)S(1)} async-done(((bf16[16,2,256]{2,1,0:T(2,128)(2,1)}), bf16[16,2,256]{2,1,0:T(2,128)(2,1)S(1)}, u32[]{:S(2)}, u32[]{:S(2)}) %all-to-all-start.1) | async-done | bytes 16416 | tf_op jit(solution)/shard_map/all_to_all | solution.py:101
  64.2 1.0 gather_fusion.2
  65.5 0.9 convolution_exponential_fusion
  66.4 1.3 multiply_reduce_fusion
  67.7 0.9 fusion.52
  68.6 0.7 fusion.65
  69.3 1.6 fusion.19
  71.2 1.8 scatter_custom_fusion.2
  73.4 9.9 %all_to_all.19 = bf16[16,2,256]{2,1,0:T(2,128)(2,1)S(1)} all-to-all(bf16[16,2,256]{2,1,0:T(2,128)(2,1)S(1)} %reshape.1809), channel_id=1, replica_groups=mesh['section'=2,'view'=8,'scene'=2] {'section','view'}, dimensions={0} | all-to-all | bytes 32768 | tf_op jit(solution)/shard_map/all_to_all | solution.py:124
  83.7 6.7 %scatter_custom_fusion.3 = f32[8,2048]{0,1:T(8,128)S(1)} fusion(s32[1024]{0:T(1024)S(1)} %bitcast.181, f32[1024,8]{1,0:T(8,128)S(1)} %copy.137, f32[]{:T(128)} %constant.123.clone.1), kind=kCustom, calls=%fused_computation.48 | custom fusion | flops 8192 | bytes 65540 | tf_op jit(solution)/shard_map/scatter-add | solution.py:130
  90.8 2.4 %fusion.58 = f32[1024,512]{1,0:T(8,128)} fusion(f32[32,512]{1,0:T(8,128)S(1)} %reshape.1631, bf16[1,32,1024]{2,1,0:T(8,128)(2,1)S(1)} %copy-done.2, f32[1024]{0:T(1024)S(1)} %copy-done.3, f32[32]{0:T(128)S(1)} %add_rsqrt_fusion), kind=kOutput, calls=%fused_computation.76 | convolution fusion | flops 201457664 | bytes 2232448 | tf_op jit(solution)/shard_map/dot_general | solution.py:133
  93.9 38.4 %psum.15 = f32[]{:T(128)} all-reduce(f32[]{:T(128)S(6)} %mul.699), channel_id=1, replica_groups=mesh['section'=2,'view'=8,'scene'=2] {'section','view','scene'}, use_global_device_ids=true, to_apply=%region_14.15 | all-reduce | flops 1 | bytes 8 | tf_op jit(solution)/shard_map/psum | solution.py:134
  132.4 0.6 convert_element_type.110
  133.0 92.0 %all-reduce.11.cloned.1.call-done = f32[1024,512]{1,0:T(8,128)} async-done(((f32[1024,512]{1,0:T(8,128)}), f32[1024,512]{1,0:T(8,128)}) %all-reduce.11.cloned.1.call-update) | async-done | bytes 2097168 | tf_op jit(solution)/shard_map/psum | solution.py:134
  224.9 3.1 %copy.158 = f32[1024,512]{1,0:T(8,128)} copy(f32[1024,512]{1,0:T(8,128)} %all-reduce.11.cloned.1.call-done) | data formatting | bytes 4194304
  (71 shorter events, 4.4 us)
Async XLA Ops:
  7.2 33.6 %copy-start = (f32[1,2,8]{2,1,0:T(2,128)S(1)}, f32[1,2,8]{2,1,0:T(2,128)}, u32[]{:S(2)}) copy-start(f32[1,2,8]{2,1,0:T(2,128)} %param.12) | copy-start | bytes 196
  7.2 33.3 %copy-start.5 = (s32[1,4]{1,0:T(1,128)S(1)}, s32[1,4]{1,0:T(1,128)}, u32[]{:S(2)}) copy-start(s32[1,4]{1,0:T(1,128)} %param.11) | copy-start | bytes 52
  7.2 33.5 %copy-start.2 = (bf16[1,32,1024]{2,1,0:T(8,128)(2,1)S(1)}, bf16[1,32,1024]{2,1,0:T(8,128)(2,1)}, u32[]{:S(2)}) copy-start(bf16[1,32,1024]{2,1,0:T(8,128)(2,1)} %param.7) | copy-start | bytes 196612
  7.2 34.1 %copy-start.1 = (bf16[1024,512]{1,0:T(8,128)(2,1)S(1)}, bf16[1024,512]{1,0:T(8,128)(2,1)}, u32[]{:S(2)}) copy-start(bf16[1024,512]{1,0:T(8,128)(2,1)} %param.9) | copy-start | bytes 3145732
  11.9 30.0 %copy-start.3 = (f32[1024]{0:T(1024)S(1)}, f32[1024]{0:T(1024)}, u32[]{:S(2)}) copy-start(f32[1024]{0:T(1024)} %param.8) | copy-start | bytes 12292
  32.1 15.6 %all-to-all-start = ((s32[16,1,64]{2,1,0:T(1,128)}), s32[16,1,64]{2,1,0:T(1,128)S(1)}, u32[]{:S(2)}, u32[]{:S(2)}) async-start(s32[16,1,64]{2,1,0:T(1,128)} %all_to_all.12), calls=%async_computation | async-start | bytes 16384 | tf_op jit(solution)/shard_map/all_to_all | solution.py:91
  41.3 15.3 %copy-start.4 = (bf16[1,4,768]{2,1,0:T(4,128)(2,1)S(1)}, bf16[1,4,768]{2,1,0:T(4,128)(2,1)}, u32[]{:S(2)}) copy-start(bf16[1,4,768]{2,1,0:T(4,128)(2,1)} %param.13) | copy-start | bytes 18436
  53.1 10.8 %all-to-all-start.1 = ((bf16[16,2,256]{2,1,0:T(2,128)(2,1)}), bf16[16,2,256]{2,1,0:T(2,128)(2,1)S(1)}, u32[]{:S(2)}, u32[]{:S(2)}) async-start(bf16[16,2,256]{2,1,0:T(2,128)(2,1)} %reshape.1807), calls=%async_computation.1 | async-start | bytes 32768 | tf_op jit(solution)/shard_map/all_to_all | solution.py:101
  56.6 168.4 %all-reduce.11.cloned.1.call-start = ((), (), s32[]{:S(2)}) async-start(), calls=%async_computation.3 | async-start | bytes 4194304 | tf_op jit(solution)/shard_map/psum | solution.py:134
Sparse Core Ops, SparseCore 0:
  93.4 131.5 all-reduce.10
where the time goes:
time: 235 us
  waiting for transfers between devices  104 us (44%)
  blocking collectives  48.4 us (21%)
  local copies, waits for them, and re-layouts  23.8 us (10%)
  other arithmetic  23.1 us (10%)
  between operations  15.1 us (6%)
  starting transfers between devices  11.9 us (5%)
  matrix products  8.56 us (4%)
    psum x1, waiting for transfers between devices, body(): lax.psum((partial_grad, part * factor), ('section', 'view', 'scene'))  92 us
    psum x1, blocking collectives, body(): lax.psum((partial_grad, part * factor), ('section', 'view', 'scene'))  38.4 us
    all_to_all x1, blocking collectives, body(): lax.all_to_all(outgoing.astype(jnp.bfloat16), ('section', 'view'), split_...  9.91 us
    all_to_all x1, starting transfers between devices, body(): lax.all_to_all(wanted_rows, ('section', 'view'), split_axis=0, concat_axi...  8.34 us
    all_to_all x1, waiting for transfers between devices, body(): lax.all_to_all(answer, ('section', 'view'), split_axis=0, concat_axis=0,...  7.22 us
    scatter-add x1, other arithmetic, body(): own = jnp.zeros((PARAMS, own_count), jnp.float32).at[:, asked.reshape(-1)...  6.69 us
    add x1, other arithmetic, body(): sorted_owner * bucket + rank  5.71 us
    all_to_all x1, waiting for transfers between devices, body(): lax.all_to_all(wanted_rows, ('section', 'view'), split_axis=0, concat_axi...  4.9 us
  transfers between devices with their start and end apart: 3, of which 3 were waited for; matrix products, arithmetic and copies ran while one was open for 1% of the time, Pallas kernels for 0%

commit v1 on v0

v1 whole, which is shorter than its diff:
```python
import functools

import jax
import jax.numpy as jnp
from jax import lax
from jax.experimental import pallas as pl
from jax.experimental.pallas import tpu as pltpu
from jax.sharding import PartitionSpec as P

PARAMS = 8
SIDE = 16
VIEWS = 2
MESH = pl.DeviceIdType.MESH
F32 = jnp.float32
BF16 = jnp.bfloat16
NN = (((1,), (0,)), ((), ()))
NT = (((1,), (1,)), ((), ()))
TN = (((0,), (0,)), ((), ()))


def mm(a, b, dims):
    return lax.dot_general(a, b, dims, preferred_element_type=F32)


def split(x):
    hi = x.astype(BF16)
    lo = (x - hi.astype(F32)).astype(BF16)
    return hi, lo


def mm2(a, x, dims):
    hi, lo = split(x)
    return mm(a, hi, dims) + mm(a, lo, dims)


def mm3(x, y, dims):
    xh, xl = split(x)
    yh, yl = split(y)
    return mm(xh, yh, dims) + mm(xh, yl, dims) + mm(xl, yh, dims)


def sigmoid(x):
    return 1.0 / (1.0 + jnp.exp(-x))


def pick(row, tokens, gpt):
    tok = row // gpt
    at = lax.broadcasted_iota(jnp.int32, (tokens, row.shape[1]), 0)
    return jnp.where(at == tok, 1.0, 0.0).astype(BF16)


def kernel(
    nsec, nview, factor,
    tok_ref, gain_ref, w_ref, list_ref, count_ref, cam_ref, want_ref,
    image_ref, grad_ref, loss_ref,
    heads, norms, lists, grads, dhead, mine, theirs, loss_mine, loss_theirs,
    s_list, r_list, s_head, r_head, s_norm, r_norm, s_grad, r_grad, s_part, r_part, s_loss, r_loss,
):
    group = nsec * nview
    sec, view, scene = lax.axis_index("section"), lax.axis_index("view"), lax.axis_index("scene")
    me = sec * nview + view
    tok_rows, width = tok_ref.shape
    outw = w_ref.shape[1]
    gpt = outw // PARAMS
    tiles, K = list_ref.shape
    tokens = group * tok_rows
    pix = SIDE * SIDE

    def peer(i):
        j = lax.rem(me + i, group)
        return j, (j // nview, lax.rem(j, nview), scene)

    partner = (sec, view, 1 - scene)

    barrier = pltpu.get_barrier_semaphore()

    @pl.loop(1, group)
    def _(i):
        pl.semaphore_signal(barrier, inc=1, device_id=peer(i)[1], device_id_type=MESH)

    pl.semaphore_signal(barrier, inc=1, device_id=partner, device_id_type=MESH)

    x = tok_ref[...].astype(F32)
    scale = lax.rsqrt(jnp.mean(x * x, axis=-1, keepdims=True) + 1e-06)
    normed = (x * scale * gain_ref[...]).astype(BF16)
    norms[me] = normed
    heads[me] = mm(normed, w_ref[...], NN).astype(BF16)
    lists[me] = list_ref[...]

    pl.semaphore_wait(barrier, group)

    def push(buf, src, send, recv, i):
        j, where = peer(i)
        return pltpu.make_async_remote_copy(
            src_ref=src, dst_ref=buf.at[me], send_sem=send.at[i], recv_sem=recv.at[me],
            device_id=where, device_id_type=MESH,
        )

    def take(buf, send, recv, j):
        pltpu.make_async_remote_copy(
            src_ref=buf.at[j], dst_ref=buf.at[j], send_sem=send.at[0], recv_sem=recv.at[j],
            device_id=partner, device_id_type=MESH,
        ).wait_recv()

    def take_all(buf, send, recv):
        @pl.loop(1, group)
        def _(i):
            take(buf, send, recv, peer(i)[0])

    @pl.loop(1, group)
    def _(i):
        push(heads, heads.at[me], s_head, r_head, i).start()

    @pl.loop(1, group)
    def _(i):
        push(lists, list_ref, s_list, r_list, i).start()

    @pl.loop(1, group)
    def _(i):
        push(norms, norms.at[me], s_norm, r_norm, i).start()

    own = jnp.concatenate([list_ref[pl.ds(b, 1), :] for b in range(tiles)], axis=1)
    hot = pick(own, tokens, gpt)
    inner = own - (own // gpt) * gpt
    at_g = lax.broadcasted_iota(jnp.int32, (gpt, tiles * K), 0)
    mask = jnp.where(at_g == inner, 1.0, 0.0)

    take_all(heads, s_head, r_head)
    table = heads[...].reshape(tokens, outw)
    picked = mm(table, hot, TN)
    rows = [
        jnp.sum(picked[p * gpt : (p + 1) * gpt] * mask, axis=0, keepdims=True)
        for p in range(PARAMS)
    ]

    place = lax.broadcasted_iota(jnp.int32, (1, pix), 1)
    across = ((place % SIDE).astype(F32) + 0.5) * (2.0 / SIDE) - 1.0
    down = ((place // SIDE).astype(F32) + 0.5) * (2.0 / SIDE) - 1.0
    ka = lax.broadcasted_iota(jnp.int32, (K, K), 0)
    kb = lax.broadcasted_iota(jnp.int32, (K, K), 1)
    lower = jnp.where(kb < ka, 1.0, 0.0).astype(BF16)
    upper = jnp.where(kb > ka, 1.0, 0.0).astype(BF16)
    ones = jnp.ones((8, pix), BF16)
    per_view = (tiles * group) // VIEWS
    slot = lax.broadcasted_iota(jnp.int32, (1, K), 1)
    zero_row = jnp.zeros((1, K), F32)

    for b in range(tiles):
        cut = slice(b * K, (b + 1) * K)
        mx, my, mz, ls, op, cr, cg, cb = [r[:, cut] for r in rows]
        vi = (me * tiles + b) // per_view
        cam = [cam_ref[vi, n] for n in range(8)]
        live = jnp.where(slot < count_ref[b], 1.0, 0.0)
        sx = jnp.tanh(cam[0] * mx + cam[1] * my + cam[2] * mz + cam[3])
        sy = jnp.tanh(cam[4] * mx + cam[5] * my + cam[6] * mz + cam[7])
        spread = jnp.exp(-2.0 * ls)
        sop = sigmoid(op)
        amp = 0.3 * sop * live
        shade = sigmoid(jnp.concatenate([cr, cg, cb], axis=0))
        shade8 = jnp.concatenate([shade, jnp.zeros((5, K), F32)], axis=0)
        cols = jnp.concatenate([sx, sy, spread, amp, jnp.zeros((K - 4, K), F32)], axis=0).T
        csx, csy, csp, camp = [cols[:, n : n + 1] for n in range(4)]
        dx = across - csx
        dy = down - csy
        r2 = dx * dx + dy * dy
        alpha = camp * jnp.exp(-0.5 * r2 * csp)
        rest = 1.0 - alpha
        trans = jnp.exp(mm2(lower, jnp.log(rest), NN))
        weight = alpha * trans
        colour = mm3(shade8, weight, NN)
        for c in range(3):
            image_ref[pl.ds(b, 1), c * pix : (c + 1) * pix] = colour[c : c + 1].astype(BF16)
        want = jnp.concatenate(
            [want_ref[pl.ds(b, 1), c * pix : (c + 1) * pix].astype(F32) for c in range(3)]
            + [jnp.zeros((5, pix), F32)],
            axis=0,
        )
        diff = colour - want
        sq = jnp.sum(diff * diff, axis=0, keepdims=True)
        part = sq[:, :K]
        for n in range(1, pix // K):
            part = part + sq[:, n * K : (n + 1) * K]
        part = part * factor
        dcol = (2.0 * factor) * diff
        dw = mm3(shade8, dcol, TN)
        dshade = mm3(dcol, weight, NT)
        dww = dw * weight
        dlogs = mm2(upper, dww, NN)
        h = dww - dlogs * alpha / rest
        s_h = mm2(ones, h, NT)[0:1]
        s_x = mm2(ones, h * dx, NT)[0:1]
        s_y = mm2(ones, h * dy, NT)[0:1]
        s_r = mm2(ones, h * r2, NT)[0:1]
        px = spread * s_x * (1.0 - sx * sx)
        py = spread * s_y * (1.0 - sy * sy)
        dcolour = dshade[0:3] * shade * (1.0 - shade)
        l0 = part.astype(BF16).astype(F32)
        l1 = (part - l0).astype(BF16).astype(F32)
        l2 = part - l0 - l1
        out = jnp.concatenate(
            [
                cam[0] * px + cam[4] * py,
                cam[1] * px + cam[5] * py,
                cam[2] * px + cam[6] * py,
                spread * s_r,
                (1.0 - sop) * s_h,
                dcolour,
                l0,
                l1,
                l2,
                jnp.zeros((5, K), F32),
            ],
            axis=0,
        )
        grads[me, :, cut] = out.astype(BF16)

    @pl.loop(1, group)
    def _(i):
        push(grads, grads.at[me], s_grad, r_grad, i).start()

    take_all(lists, s_list, r_list)
    dhead[...] = jnp.zeros_like(dhead)
    loss_mine[...] = jnp.zeros_like(loss_mine)

    @pl.loop(0, group)
    def _(j):
        row = jnp.concatenate([lists[j, pl.ds(b, 1), :] for b in range(tiles)], axis=1)
        where = pick(row, tokens, gpt)
        g = row - (row // gpt) * gpt
        fits = lax.broadcasted_iota(jnp.int32, (gpt, tiles * K), 0) == g

        @pl.when(j != me)
        def _():
            take(grads, s_grad, r_grad, j)

        got = grads[j].astype(F32)
        spreadout = jnp.concatenate(
            [jnp.where(fits, got[p : p + 1], 0.0).astype(BF16) for p in range(PARAMS)], axis=0
        )
        dhead[...] += mm(where, spreadout, NT)
        lossy = got[8:9] + got[9:10] + got[10:11]
        for b in range(tiles):
            loss_mine[0:1, :] += lossy[:, b * K : (b + 1) * K]

    take_all(norms, s_norm, r_norm)
    loss_copy = pltpu.make_async_remote_copy(
        src_ref=loss_mine, dst_ref=loss_theirs, send_sem=s_loss, recv_sem=r_loss,
        device_id=partner, device_id_type=MESH,
    )
    dh = dhead[...].astype(BF16)
    dhead_rows = 256
    chunks = width // dhead_rows

    def part_copy(n):
        span = pl.ds(n * dhead_rows, dhead_rows)
        return pltpu.make_async_remote_copy(
            src_ref=mine.at[span], dst_ref=theirs.at[span],
            send_sem=s_part.at[n], recv_sem=r_part.at[n],
            device_id=partner, device_id_type=MESH,
        )

    for n in range(chunks):
        a = norms[:, :, n * dhead_rows : (n + 1) * dhead_rows].reshape(tokens, dhead_rows)
        mine[n * dhead_rows : (n + 1) * dhead_rows, :] = mm(a, dh, TN).astype(BF16)
        if n == 0:
            loss_copy.start()
        else:
            part_copy(n - 1).start()
    part_copy(chunks - 1).start()

    for n in range(chunks):
        part_copy(n).wait_recv()
        span = slice(n * dhead_rows, (n + 1) * dhead_rows)
        grad_ref[span, :] = mine[span, :].astype(F32) + theirs[span, :].astype(F32)
    loss_copy.wait_recv()
    loss_ref[...] = jnp.broadcast_to(
        jnp.sum(loss_mine[...] + loss_theirs[...], keepdims=True), loss_ref.shape
    )

    loss_copy.wait_send()
    for n in range(chunks):
        part_copy(n).wait_send()

    @pl.loop(1, group)
    def _(i):
        push(heads, heads.at[me], s_head, r_head, i).wait_send()
        push(lists, list_ref, s_list, r_list, i).wait_send()
        push(norms, norms.at[me], s_norm, r_norm, i).wait_send()
        push(grads, grads.at[me], s_grad, r_grad, i).wait_send()


def solution(mesh):
    nsec, nview, nscene = mesh.shape["section"], mesh.shape["view"], mesh.shape["scene"]
    group = nsec * nview

    def body(tokens, norm_gain, head_weight, tile_lists, tile_counts, cameras, targets):
        tok_rows, width = tokens.shape[1:]
        outw = head_weight.shape[1]
        tiles, K = tile_lists.shape[1:]
        factor = 1.0 / (nscene * tiles * group)
        vmem = pl.BlockSpec(memory_space=pltpu.VMEM)
        smem = pl.BlockSpec(memory_space=pltpu.SMEM)
        dma = pltpu.SemaphoreType.DMA
        image, grad, loss = pl.pallas_call(
            functools.partial(kernel, nsec, nview, factor),
            out_shape=(
                jax.ShapeDtypeStruct((tiles, targets.shape[2]), BF16),
                jax.ShapeDtypeStruct((width, outw), F32),
                jax.ShapeDtypeStruct((8, 128), F32),
            ),
            in_specs=[vmem, vmem, vmem, vmem, smem, smem, vmem],
            out_specs=(vmem, vmem, vmem),
            scratch_shapes=[
                pltpu.VMEM((group, tok_rows, outw), BF16),
                pltpu.VMEM((group, tok_rows, width), BF16),
                pltpu.VMEM((group, tiles, K), jnp.int32),
                pltpu.VMEM((group, 16, tiles * K), BF16),
                pltpu.VMEM((group * tok_rows, outw), F32),
                pltpu.VMEM((width, outw), BF16),
                pltpu.VMEM((width, outw), BF16),
                pltpu.VMEM((8, K), F32),
                pltpu.VMEM((8, K), F32),
            ]
            + [dma((group,))] * 8
            + [dma((width // 256,))] * 2
            + [dma, dma],
            compiler_params=pltpu.CompilerParams(
                collective_id=0, has_side_effects=True, vmem_limit_bytes=60 * 1024 * 1024
            ),
        )(
            tokens[0], norm_gain[None], head_weight, tile_lists[0], tile_counts[0], cameras[0],
            targets[0],
        )
        return image[None], grad, loss[0, 0]

    in_specs = (
        P("scene", ("section", "view"), None),
        P(),
        P(),
        P("scene", ("section", "view"), None),
        P("scene", ("section", "view")),
        P("scene", None, None),
        P("scene", ("section", "view"), None),
    )
    out_specs = (P("scene", ("section", "view"), None), P(), P())
    return jax.shard_map(body, mesh=mesh, in_specs=in_specs, out_specs=out_specs, check_vma=False)
```

time: 235 us -> 68.7 us (0.29)
  waiting for transfers between devices: 104 us -> 0 us
  Pallas kernels: 0 us -> 62.2 us
  blocking collectives: 48.4 us -> 0 us
  other arithmetic: 23.1 us -> 0 us
  local copies, waits for them, and re-layouts: 23.8 us -> 5.56 us
  between operations: 15.1 us -> 0.64 us
  starting transfers between devices: 11.9 us -> 0 us
  matrix products: 8.56 us -> 0 us
    psum x1 -> x0, waiting for transfers between devices: 92 us -> none  [body(): lax.psum((partial_grad, part * factor), ('section', 'view', 'scene'))]
    pallas_call x0 -> x1, Pallas kernels: none -> 62.2 us  [body(): pl.pallas_call(functools.partial(kernel, nsec, nview, factor), out_shape=...]
    psum x1 -> x0, blocking collectives: 38.4 us -> none  [body(): lax.psum((partial_grad, part * factor), ('section', 'view', 'scene'))]
    all_to_all x2 -> x0, waiting for transfers between devices: 12.1 us -> none  [the longest x1 7.22 us: body(): lax.all_to_all(answer, ('section', 'view'), split_axis=0, concat_axis=0,...]
    all_to_all x2 -> x0, starting transfers between devices: 11.8 us -> none  [the longest x1 8.34 us: body(): lax.all_to_all(wanted_rows, ('section', 'view'), split_axis=0, concat_axi...]
    all_to_all x1 -> x0, blocking collectives: 9.91 us -> none  [body(): lax.all_to_all(outgoing.astype(jnp.bfloat16), ('section', 'view'), split_...]
    gather x6 -> x0, local copies, waits for them, and re-layouts: 8.69 us -> none  [the longest x1 3.51 us: body(): sorted_owner = owner[order]]
    dot_general x8 -> x0, matrix products: 8.56 us -> none  [the longest x3 2.84 us: composite(): jnp.einsum('bkp,cbk->bcp', weight, jax.nn.sigmoid(values[5:8]), precision...]
  transfers between devices with their start and end apart: 3 -> 0, of which waited for: 3 -> 0; matrix products, arithmetic and copies ran while one was open for 1% -> 0% of each run, Pallas kernels for 0% -> 0%
where the time goes in v1:
time: 68.7 us; the launch traced here: 68.4 us
  Pallas kernels  62.2 us (91%)
  local copies, waits for them, and re-layouts  5.56 us (8%)
    pallas_call x1, Pallas kernels, body(): pl.pallas_call(functools.partial(kernel, nsec, nview, factor), out_shape=...  62.2 us
    unnamed x2, local copies, waits for them, and re-layouts  4.37 us

profile of v1, /device:TPU:0, one launch (start us, length us, event | category | flops | bytes accessed | tf_op | source)
XLA Modules:
  0.0 68.4 jit_solution(14421559302748882953)
XLA Ops:
  0.6 62.2 %shard_map.94 = (bf16[4,768]{1,0:T(4,128)(2,1)}, f32[1024,512]{1,0:T(8,128)}, f32[8,128]{1,0:T(8,128)}) custom-call(bf16[32,1024]{1,0:T(8,128)(2,1)} %bitcast.8, f32[1,1024]{1,0:T(1,128)} %bitcast.11, bf16[1024,512]{1,0:T(8,128)(2,1)} %w_ref.1, s32[4,128]{1,0:T(4,128)} %bitcast.12, s32[4]{0:T(128)} %bitcast.14, f32[2,8]{1,0:T(2,128)} %bitcast.13, ...), custom_call_target="tpu_custom_call" | custom-call | tf_op jit(solution)/shard_map/pallas_call | solution.py:304
  62.8 1.2 %slice.3 = f32[1,1]{1,0:T(1,128)} slice(f32[8,128]{1,0:T(8,128)} %get-tuple-element.8), slice={[0:1], [0:1]} | slice | bytes 8 | tf_op jit(solution)/shard_map/slice | solution.py:334
  64.0 1.3 %copy.12 = bf16[1,4,768]{2,1,0:T(4,128)(2,1)} copy(bf16[1,4,768]{2,1,0:T(4,128)(2,1)} %bitcast.10) | data formatting | bytes 12288
  65.3 3.1 %copy.13 = f32[1024,512]{1,0:T(8,128)} copy(f32[1024,512]{1,0:T(8,128)} %get-tuple-element.13) | data formatting | bytes 4194304

commit v2 on v1

--- a/solution.py
+++ b/solution.py
@@ -70,6 +70,14 @@
         j = lax.rem(me + i, group)
         return j, (j // nview, lax.rem(j, nview), scene)
 
+    def along_view(i):
+        v = lax.rem(view + i, nview)
+        return sec * nview + v, (sec, v, scene)
+
+    def along_section(i):
+        s = lax.rem(sec + i, nsec)
+        return s, (s, view, scene)
+
     partner = (sec, view, 1 - scene)
 
     barrier = pltpu.get_barrier_semaphore()
@@ -107,17 +115,58 @@
         def _(i):
             take(buf, send, recv, peer(i)[0])
 
-    @pl.loop(1, group)
-    def _(i):
-        push(heads, heads.at[me], s_head, r_head, i).start()
+    def first(buf, send, recv, i):
+        return pltpu.make_async_remote_copy(
+            src_ref=buf.at[me], dst_ref=buf.at[me], send_sem=send.at[i], recv_sem=recv.at[me],
+            device_id=along_view(i)[1], device_id_type=MESH,
+        )
+
+    def relay(buf, send, recv, i, k):
+        j = along_view(i)[0]
+        return pltpu.make_async_remote_copy(
+            src_ref=buf.at[j], dst_ref=buf.at[j],
+            send_sem=send.at[nview + i * (nsec - 1) + k - 1], recv_sem=recv.at[j],
+            device_id=along_section(k)[1], device_id_type=MESH,
+        )
+
+    def spread_own(buf, send, recv):
+        for k in range(1, nsec):
+            relay(buf, send, recv, 0, k).start()
+
+        @pl.loop(1, nview)
+        def _(i):
+            first(buf, send, recv, i).start()
+
+    def spread_rest(buf, send, recv):
+        @pl.loop(1, nview)
+        def _(i):
+            take(buf, send, recv, along_view(i)[0])
+            for k in range(1, nsec):
+                relay(buf, send, recv, i, k).start()
+
+    def collect(buf, send, recv):
+        for k in range(1, nsec):
+            s = along_section(k)[0]
+
+            @pl.loop(0, nview)
+            def _(i):
+                take(buf, send, recv, s * nview + lax.rem(view + i, nview))
+
+    def drain(buf, send, recv):
+        @pl.loop(1, nview)
+        def _(i):
+            first(buf, send, recv, i).wait_send()
+
+        @pl.loop(0, nview)
+        def _(i):
+            for k in range(1, nsec):
+                relay(buf, send, recv, i, k).wait_send()
 
     @pl.loop(1, group)
     def _(i):
         push(lists, list_ref, s_list, r_list, i).start()
 
-    @pl.loop(1, group)
-    def _(i):
-        push(norms, norms.at[me], s_norm, r_norm, i).start()
+    spread_own(heads, s_head, r_head)
 
     own = jnp.concatenate([list_ref[pl.ds(b, 1), :] for b in range(tiles)], axis=1)
     hot = pick(own, tokens, gpt)
@@ -125,7 +174,9 @@
     at_g = lax.broadcasted_iota(jnp.int32, (gpt, tiles * K), 0)
     mask = jnp.where(at_g == inner, 1.0, 0.0)
 
-    take_all(heads, s_head, r_head)
+    spread_rest(heads, s_head, r_head)
+    collect(heads, s_head, r_head)
+    spread_own(norms, s_norm, r_norm)
     table = heads[...].reshape(tokens, outw)
     picked = mm(table, hot, TN)
     rows = [
@@ -218,6 +269,7 @@
     def _(i):
         push(grads, grads.at[me], s_grad, r_grad, i).start()
 
+    spread_rest(norms, s_norm, r_norm)
     take_all(lists, s_list, r_list)
     dhead[...] = jnp.zeros_like(dhead)
     loss_mine[...] = jnp.zeros_like(loss_mine)
@@ -242,7 +294,7 @@
         for b in range(tiles):
             loss_mine[0:1, :] += lossy[:, b * K : (b + 1) * K]
 
-    take_all(norms, s_norm, r_norm)
+    collect(norms, s_norm, r_norm)
     loss_copy = pltpu.make_async_remote_copy(
         src_ref=loss_mine, dst_ref=loss_theirs, send_sem=s_loss, recv_sem=r_loss,
         device_id=partner, device_id_type=MESH,
@@ -271,7 +323,7 @@
     for n in range(chunks):
         part_copy(n).wait_recv()
         span = slice(n * dhead_rows, (n + 1) * dhead_rows)
-        grad_ref[span, :] = mine[span, :].astype(F32) + theirs[span, :].astype(F32)
+        grad_ref[span, :] = (mine[span, :].astype(F32) + theirs[span, :].astype(F32)).astype(BF16)
     loss_copy.wait_recv()
     loss_ref[...] = jnp.broadcast_to(
         jnp.sum(loss_mine[...] + loss_theirs[...], keepdims=True), loss_ref.shape
@@ -283,10 +335,11 @@
 
     @pl.loop(1, group)
     def _(i):
-        push(heads, heads.at[me], s_head, r_head, i).wait_send()
         push(lists, list_ref, s_list, r_list, i).wait_send()
-        push(norms, norms.at[me], s_norm, r_norm, i).wait_send()
         push(grads, grads.at[me], s_grad, r_grad, i).wait_send()
+
+    drain(heads, s_head, r_head)
+    drain(norms, s_norm, r_norm)
 
 
 def solution(mesh):
@@ -305,7 +358,7 @@
             functools.partial(kernel, nsec, nview, factor),
             out_shape=(
                 jax.ShapeDtypeStruct((tiles, targets.shape[2]), BF16),
-                jax.ShapeDtypeStruct((width, outw), F32),
+                jax.ShapeDtypeStruct((width, outw), BF16),
                 jax.ShapeDtypeStruct((8, 128), F32),
             ),
             in_specs=[vmem, vmem, vmem, vmem, smem, smem, vmem],
@@ -321,7 +374,9 @@
                 pltpu.VMEM((8, K), F32),
                 pltpu.VMEM((8, K), F32),
             ]
-            + [dma((group,))] * 8
+            + [dma((group,))] * 2
+            + [dma((nview * nsec,)), dma((group,))] * 2
+            + [dma((group,))] * 2
             + [dma((width // 256,))] * 2
             + [dma, dma],
             compiler_params=pltpu.CompilerParams(
@@ -331,7 +386,7 @@
             tokens[0], norm_gain[None], head_weight, tile_lists[0], tile_counts[0], cameras[0],
             targets[0],
         )
-        return image[None], grad, loss[0, 0]
+        return image[None], grad.astype(F32), loss[0, 0]
 
     in_specs = (
         P("scene", ("section", "view"), None),

time: 68.7 us -> 57.9 us (0.84)
  the two profiles are of different devices: /device:TPU:0 before, /device:TPU:27 now
where the time goes in v2:
time: 57.9 us; the launch traced here: 57.7 us
  Pallas kernels  52.4 us (91%)
  other arithmetic  2.83 us (5%)
  local copies, waits for them, and re-layouts  1.79 us (3%)
  between operations  0.65 us (1%)
    pallas_call x1, Pallas kernels, body(): pl.pallas_call(functools.partial(kernel, nsec, nview, factor), out_shape=...  52.4 us
    convert_element_type x1, other arithmetic, body(): return (image[None], grad.astype(F32), loss[0, 0])  2.83 us
    slice x1, local copies, waits for them, and re-layouts, body(): return (image[None], grad.astype(F32), loss[0, 0])  1.2 us

profile of v2, /device:TPU:27, one launch (start us, length us, event | category | flops | bytes accessed | tf_op | source)
XLA Modules:
  0.0 57.7 jit_solution(7469781707545154565)
XLA Ops:
  0.6 52.4 %shard_map.94 = (bf16[4,768]{1,0:T(4,128)(2,1)}, bf16[1024,512]{1,0:T(8,128)(2,1)}, f32[8,128]{1,0:T(8,128)}) custom-call(bf16[32,1024]{1,0:T(8,128)(2,1)} %bitcast.8, f32[1,1024]{1,0:T(1,128)} %bitcast.11, bf16[1024,512]{1,0:T(8,128)(2,1)} %w_ref.1, s32[4,128]{1,0:T(4,128)} %bitcast.12, s32[4]{0:T(128)} %bitcast.14, f32[2,8]{1,0:T(2,128)} %bitcast.13, ...), custom_call_target="tpu_custom_call" | custom-call | tf_op jit(solution)/shard_map/pallas_call | solution.py:357
  53.0 0.0 copy-start
  53.0 1.2 %slice.3 = f32[1,1]{1,0:T(1,128)} slice(f32[8,128]{1,0:T(8,128)} %get-tuple-element.8), slice={[0:1], [0:1]} | slice | bytes 8 | tf_op jit(solution)/shard_map/slice | solution.py:389
  54.2 2.8 %convert_element_type.3 = f32[1024,512]{1,0:T(8,128)} convert(bf16[1024,512]{1,0:T(8,128)(2,1)} %get-tuple-element.7) | non-fusion elementwise | flops 524288 | bytes 3145728 | tf_op jit(solution)/shard_map/convert_element_type | solution.py:389
  57.1 0.0 copy-done
  57.1 0.6 %copy.11 = bf16[1,4,768]{2,1,0:T(4,128)(2,1)} copy(bf16[1,4,768]{2,1,0:T(4,128)(2,1)S(1)} %bitcast.10) | data formatting | bytes 12288
Async XLA Ops:
  53.0 4.0 %copy-start = (bf16[4,768]{1,0:T(4,128)(2,1)S(1)}, bf16[4,768]{1,0:T(4,128)(2,1)}, u32[]{:S(2)}) copy-start(bf16[4,768]{1,0:T(4,128)(2,1)} %get-tuple-element.6) | copy-start | bytes 18436
